TPU v7x, 32 devices: a whole 2x2x4 slice. The times are simulated.
32 devices in a mesh: section: 8 (over y, x, core), tensor: 4 (over z).
Axes of the slice: x: 2, y: 2, z: 4, core: 2. Of those that a mesh axis runs over, the one named last changes fastest.
Arguments:
- frozen: bfloat16 [8, 14336, 2048], P('section', 'tensor'), may hold values from -1 to 1, as said below
- adapter_a: bfloat16 [8, 8, 14336], P('section', None, 'tensor'), may hold values from -0.119628906 to 0.119628906
- adapter_b: bfloat16 [8, 16, 2048], P('section'), may hold values from -0.22460938 to 0.22460938
- magnitude: float32 [8, 2048], P('section'), may hold values from 0.5 to 2
- hidden_fwd: bfloat16 [8, 128, 14336], P('section', None, 'tensor'), may hold values from -6 to 6
- carried: bfloat16 [8, 256, 2048], P('section', 'tensor'), may hold values from -6 to 6
- embedded: bfloat16 [256, 4096], P('tensor'), may hold values from -6 to 6
- hidden_bwd: bfloat16 [8, 128, 14336], P('section', None, 'tensor'), may hold values from -6 to 6
- returned: bfloat16 [8, 256, 2048], P('section', 'tensor'), may hold values from -1.5 to 1.5
- head_grad: bfloat16 [256, 4096], P('tensor'), may hold values from -1.5 to 1.5
Outputs:
- section_out: bfloat16 [8, 256, 2048], P('section', 'tensor')
- grad_magnitude: float32 [8, 2048], P('section')
- grad_a: float32 [8, 8, 14336], P('section', None, 'tensor')
- grad_b: float32 [8, 16, 2048], P('section')
- hidden_grad: bfloat16 [8, 128, 14336], P('section', None, 'tensor')
Inputs may be any that keep to these rules, and one draw needn't show every extreme that they name: frozen projection weights.
All inputs are finite; a program needn't handle non-finite values.
Results may differ from a plain program's by a relative error of at most 0.0057.
Values may be sent and summed in bfloat16 or wider, within the bound.
No kernel may reach another device: no remote copies, remote signals or barrier semaphores. Data moves between devices by JAX's collectives and lax.ppermute only.
A program may use at most 128 MiB of HBM per device.

v0:
```python
import jax
import jax.numpy as jnp
from jax import lax
from jax.sharding import PartitionSpec as P

epsilon = 1e-06


def swapped(array, axis, apart):
    return lax.ppermute(array, axis, [(i, i ^ 1 << apart) for i in range(lax.axis_size(axis))])


def from_behind(array, axis, by):
    count = lax.axis_size(axis)
    pairs = [(i, i + by) for i in range(count) if 0 <= i + by < count]
    return lax.ppermute(array, axis, pairs)


def column_norms(squares):
    return jnp.sqrt(lax.psum(squares, "tensor") + epsilon)


def forward_rows(term_fn, own_rows):
    return lax.psum_scatter(
        term_fn(jnp.int32(0), own_rows * lax.axis_size("tensor")),
        "tensor",
        scatter_dimension=0,
        tiled=True,
    )


def local(
    frozen,
    adapter_a,
    adapter_b,
    magnitude,
    hidden_fwd,
    carried,
    embedded,
    hidden_bwd,
    returned,
    head_grad,
):
    base_w = frozen[0]
    fac_half = adapter_a[0]
    fac_b = adapter_b[0]
    mag = magnitude[0]
    own_rows = carried.shape[1]
    slot_id = lax.axis_index("section")
    slot_count = lax.axis_size("section")
    half = slot_id % 2
    first_half = half == 0
    fwd_other, bwd_other, fac_other = swapped(
        (hidden_fwd[0], hidden_bwd[0], fac_half), "section", 0
    )

    def in_order(own, other):
        return jnp.concatenate(
            [jnp.where(first_half, own, other), jnp.where(first_half, other, own)], axis=0
        )

    hid_fwd = in_order(hidden_fwd[0], fwd_other)
    hid_bwd = in_order(hidden_bwd[0], bwd_other)
    fac_a = in_order(fac_half, fac_other)
    width = base_w.shape[1]
    arriving = from_behind(carried[0], "section", 2)
    embed_cols = lax.dynamic_slice_in_dim(embedded, half * width, width, 1)
    inflow = jnp.where(slot_id < 2, embed_cols, arriving)
    coming = from_behind(returned[0], "section", -2)
    head_cols = lax.dynamic_slice_in_dim(head_grad, half * width, width, 1)
    cotangent = jnp.where(slot_id >= slot_count - 2, head_cols, coming)
    merged = (
        base_w.astype(jnp.float32)
        + jnp.einsum("rf,rd->fd", fac_a, fac_b, preferred_element_type=jnp.float32)
    ).astype(jnp.bfloat16)
    merged_f = merged.astype(jnp.float32)
    squares = jnp.sum(merged_f * merged_f, axis=0)
    low_part = jnp.einsum("tf,rf->tr", hid_bwd, fac_a, preferred_element_type=jnp.float32)
    low = lax.psum(low_part, "tensor").astype(jnp.bfloat16)
    col_norms = column_norms(squares)
    col_scale = mag / col_norms

    def scaled_term(offset, amount):
        return jnp.dot(hid_fwd, merged, preferred_element_type=jnp.float32) * col_scale

    projected = forward_rows(scaled_term, own_rows)
    section_out = (inflow.astype(jnp.float32) + projected).astype(jnp.bfloat16)
    all_rows = hid_bwd.shape[0]
    cot_block = lax.all_gather(cotangent, "tensor", axis=0, tiled=True)
    scaled_cot = (cot_block.astype(jnp.float32) * col_scale).astype(jnp.bfloat16)
    hid_part = jnp.einsum("td,fd->tf", scaled_cot, merged, preferred_element_type=jnp.float32)
    hid_acc = hid_part
    adapt_part = jnp.einsum("td,rd->tr", scaled_cot, fac_b, preferred_element_type=jnp.float32)
    adapt_acc = adapt_part
    grad_b_acc = jnp.einsum("tr,td->rd", low, scaled_cot, preferred_element_type=jnp.float32)
    recomputed = jnp.dot(hid_bwd, merged, preferred_element_type=jnp.float32)
    mag_acc = jnp.sum(cot_block.astype(jnp.float32) * recomputed, axis=0)
    hid_acc, adapt_acc, grad_b_acc, mag_acc = (hid_acc, adapt_acc, grad_b_acc, mag_acc)
    half_rows = all_rows // 2
    send_hid = lax.dynamic_slice_in_dim(hid_acc, (1 - half) * half_rows, half_rows, 0)
    got_hid, got_adapt = swapped((send_hid, adapt_acc), "section", 0)
    own_hid = lax.dynamic_slice_in_dim(hid_acc, half * half_rows, half_rows, 0)
    hidden_grad = (own_hid + got_hid).astype(jnp.bfloat16)
    adapter_cot = (adapt_acc + got_adapt).astype(jnp.bfloat16)
    rank_half = fac_half.shape[0]
    own_cot = lax.dynamic_slice_in_dim(adapter_cot, half * rank_half, rank_half, 1)
    grad_a = jnp.einsum("tr,tf->rf", own_cot, hid_bwd, preferred_element_type=jnp.float32)
    grad_mag = lax.psum(mag_acc, "tensor") / col_norms
    return (section_out[None], grad_mag[None], grad_a[None], grad_b_acc[None], hidden_grad[None])


def solution(mesh):
    placed = (
        P("section", "tensor", None),
        P("section", None, "tensor"),
        P("section", None, None),
        P("section", None),
        P("section", None, "tensor"),
        P("section", "tensor", None),
        P("tensor", None),
        P("section", None, "tensor"),
        P("section", "tensor", None),
        P("tensor", None),
    )
    return jax.shard_map(
        local,
        mesh=mesh,
        in_specs=placed,
        out_specs=(
            P("section", "tensor", None),
            P("section", None),
            P("section", None, "tensor"),
            P("section", None, None),
            P("section", None, "tensor"),
        ),
        check_vma=False,
    )
```

profile of v0, /device:TPU:0, one launch (start us, length us, event | category | flops | bytes accessed | tf_op | source)
XLA Modules:
  0.0 143.7 jit_solution(12849420476507222453)
XLA Ops:
  7.9 1.3 collective-permute-start.3
  9.7 0.8 broadcast_select_fusion.5
  10.5 11.0 %multiply_reduce_fusion = (f32[2048]{0:T(1024)S(1)}, bf16[3584,2048]{1,0:T(8,128)(2,1)}) fusion(bf16[1,16,2048]{2,1,0:T(8,128)(2,1)S(1)} %copy-done, bf16[8,3584]{1,0:T(8,128)(2,1)S(1)} %get-tuple-element.13, bf16[8,3584]{1,0:T(8,128)(2,1)S(1)} %get-tuple-element.12, bf16[1,3584,2048]{2,1,0:T(8,128)(2,1)} %param.10), kind=kOutput, calls=%fused_computation.2 | convolution fusion | flops 279148544 | bytes 29548544 | tf_op jit(solution)/shard_map/rf,rd->fd/dot_general | solution.py:74
  21.5 0.8 dynamic-slice_select_fusion
  22.4 1.3 broadcast_select_fusion.1
  23.7 0.6 fusion.12
  24.6 0.9 copy-done.5
  25.5 1.0 broadcast_select_fusion.3
  26.6 27.4 %all-gather.2.cloned.1.call-done = bf16[256,2048]{1,0:T(8,128)(2,1)} async-done(((bf16[64,2048]{1,0:T(8,128)(2,1)}), bf16[256,2048]{1,0:T(8,128)(2,1)}) %all-gather.2.cloned.1.call-update) | async-done | bytes 1048592 | tf_op jit(solution)/shard_map/all_gather | solution.py:89
  54.0 9.7 %fusion.5 = f32[2048]{0:T(1024)S(1)} fusion(bf16[3584,2048]{1,0:T(8,128)(2,1)} %get-tuple-element.17, bf16[256,2048]{1,0:T(8,128)(2,1)} %all-gather.2.cloned.1.call-done, bf16[128,3584]{1,0:T(8,128)(2,1)} %copy-done.8, bf16[128,3584]{1,0:T(8,128)(2,1)S(1)} %get-tuple-element.8), kind=kOutput, calls=%fused_computation.14 | convolution fusion | flops 3763337216 | bytes 17571840 | tf_op jit(solution)/shard_map/dot_general | solution.py:96
  63.7 19.6 %all-reduce = (f32[2048]{0:T(1024)S(1)}, f32[2048]{0:T(1024)S(1)}, bf16[256,16]{1,0:T(8,128)(2,1)S(1)}) all-reduce(f32[2048]{0:T(1024)S(1)} %get-tuple-element.16, f32[2048]{0:T(1024)S(1)} %fusion.5, f32[256,16]{1,0:T(8,128)S(1)} %fusion.12), channel_id=1, replica_groups=mesh['section'=8,'tensor'=4] {'tensor'}, use_global_device_ids=true, to_apply=%region_1.2 | all-reduce | flops 8192 | bytes 57344 | tf_op jit(solution)/shard_map/psum | solution.py:20
  83.3 0.6 fusion.18
  83.9 8.9 %convolution_multiply_fusion.1 = f32[256,2048]{1,0:T(8,128)} fusion(bf16[3584,2048]{1,0:T(8,128)(2,1)} %get-tuple-element.17, bf16[128,3584]{1,0:T(8,128)(2,1)S(1)} %copy-done.9, bf16[128,3584]{1,0:T(8,128)(2,1)S(1)} %get-tuple-element.10, f32[2048]{0:T(1024)S(1)} %get-tuple-element.15), kind=kOutput, calls=%fused_computation.5 | convolution fusion | flops 3762290688 | bytes 18620416 | tf_op jit(solution)/shard_map/dot_general | solution.py:84
  92.9 1.2 copy-done.3
  94.1 7.7 %fusion.7 = f32[256,3584]{1,0:T(8,128)S(1)} fusion(bf16[3584,2048]{1,0:T(8,128)(2,1)} %get-tuple-element.17, bf16[256,2048]{1,0:T(8,128)(2,1)S(1)} %copy-done.3, f32[2048]{0:T(1024)S(1)} %get-tuple-element.15), kind=kOutput, calls=%fused_computation.20 | convolution fusion | flops 3759669248 | bytes 19406848 | tf_op jit(solution)/shard_map/td,fd->tf/dot_general | solution.py:91
  101.8 1.8 %copy-done.1 = f32[256,3584]{1,0:T(8,128)} copy-done((f32[256,3584]{1,0:T(8,128)}, f32[256,3584]{1,0:T(8,128)S(1)}, u32[]{:S(2)}) %copy-start.1) | copy-done | bytes 3670040
  103.6 1.4 constant_dynamic-slice_fusion
  105.0 3.4 %collective-permute-start = (bf16[64,2048]{1,0:T(8,128)(2,1)S(1)}, bf16[64,2048]{1,0:T(8,128)(2,1)S(1)}, u32[]{:S(2)}, u32[]{:S(2)}) collective-permute-start(bf16[64,2048]{1,0:T(8,128)(2,1)S(1)} %bitcast.41), channel_id=1, source_target_pairs={{0,8},{4,12},{8,16},{12,20},{16,24},{20,28},{1,9},{5,13},{9,17},{1... | collective-permute-start | bytes 786440 | tf_op jit(solution)/shard_map/ppermute | solution.py:16
  109.0 0.9 convolution_bitcast_fusion.1
  109.9 2.2 %convolution_bitcast_fusion = f32[1,8,3584]{2,1,0:T(8,128)} fusion(bf16[128,3584]{1,0:T(8,128)(2,1)} %copy-done.8, bf16[128,3584]{1,0:T(8,128)(2,1)S(1)} %copy-done.7, f32[256,16]{0,1:T(8,128)S(1)} %collective-permute-done.5, s32[]{:T(128)S(6)} %select_n.80, f32[256,16]{0,1:T(8,128)S(1)} %fusion.10), kind=kOutput, calls=%fused_computation.3 | convolution fusion | flops 18354176 | bytes 1966084 | tf_op jit(solution)/shard_map/tr,tf->rf/dot_general | solution.py:107
  112.2 1.2 fusion.6
  113.3 1.2 collective-permute-done
  114.5 20.4 %reduce-scatter.2.cloned.1.call-done = f32[64,2048]{1,0:T(8,128)} async-done(((f32[256,2048]{1,0:T(8,128)}), f32[64,2048]{1,0:T(8,128)}) %reduce-scatter.2.cloned.1.call-update) | async-done | bytes 524304 | tf_op jit(solution)/shard_map/reduce_scatter | solution.py:24
  135.0 1.8 %fusion.13 = bf16[1,64,2048]{2,1,0:T(8,128)(2,1)} fusion(f32[64,2048]{1,0:T(8,128)} %reduce-scatter.2.cloned.1.call-done, bf16[64,2048]{1,0:T(8,128)(2,1)S(1)} %collective-permute-done, bf16[64,4096]{1,0:T(8,128)(2,1)S(1)} %copy-done.11, s32[]{:T(128)S(6)} %select_n.68, pred[]{:T(512)S(6)} %lt.22), kind=kLoop, calls=%fused_computation.24 | loop fusion | flops 524288 | bytes 1310725 | tf_op jit(solution)/shard_map/broadcast_in_dim | solution.py:109
  (41 shorter events, 2.2 us)
Async XLA Ops:
  7.2 3.3 %copy-start = (bf16[1,16,2048]{2,1,0:T(8,128)(2,1)S(1)}, bf16[1,16,2048]{2,1,0:T(8,128)(2,1)}, u32[]{:S(2)}) copy-start(bf16[1,16,2048]{2,1,0:T(8,128)(2,1)} %param.12) | copy-start | bytes 196612
  7.2 46.8 %all-gather.2.cloned.1.call-start = ((), (), s32[]{:S(2)}) async-start(), calls=%async_computation.2 | async-start | bytes 1310720 | tf_op jit(solution)/shard_map/all_gather | solution.py:89
  7.2 2.4 %collective-permute-start.2 = (bf16[8,3584]{1,0:T(8,128)(2,1)}, bf16[8,3584]{1,0:T(8,128)(2,1)S(1)}, u32[]{:S(2)}, u32[]{:S(2)}) collective-permute-start(bf16[8,3584]{1,0:T(8,128)(2,1)} %bitcast.37), channel_id=1, source_target_pairs={{0,4},{4,0},{8,12},{12,8},{16,20},{20,16},{24,28},{28,24},{1,5},{5... | collective-permute-start | bytes 172040 | tf_op jit(solution)/shard_map/ppermute | solution.py:10
  7.8 16.5 %collective-permute-start.1 = (bf16[128,3584]{1,0:T(8,128)(2,1)}, bf16[128,3584]{1,0:T(8,128)(2,1)S(1)}, u32[]{:S(2)}, u32[]{:S(2)}) collective-permute-start(bf16[128,3584]{1,0:T(8,128)(2,1)} %bitcast.36), channel_id=1, source_target_pairs={{0,4},{4,0},{8,12},{12,8},{16,20},{20,16},{24,28},{28,24},{1,5},{5... | collective-permute-start | bytes 2752520 | tf_op jit(solution)/shard_map/ppermute | solution.py:10
  7.9 13.6 %collective-permute-start.3 = (bf16[64,2048]{1,0:T(8,128)(2,1)}, bf16[64,2048]{1,0:T(8,128)(2,1)S(1)}, u32[]{:S(2)}, u32[]{:S(2)}) collective-permute-start(bf16[64,2048]{1,0:T(8,128)(2,1)} %bitcast.40), channel_id=1, source_target_pairs={{8,0},{12,4},{16,8},{20,12},{24,16},{28,20},{9,1},{13,5},{17,9},{2... | collective-permute-start | bytes 786440 | tf_op jit(solution)/shard_map/ppermute | solution.py:16
  9.2 13.2 %collective-permute-start.4 = (bf16[128,3584]{1,0:T(8,128)(2,1)}, bf16[128,3584]{1,0:T(8,128)(2,1)}, u32[]{:S(2)}, u32[]{:S(2)}) collective-permute-start(bf16[128,3584]{1,0:T(8,128)(2,1)} %bitcast.35), channel_id=1, source_target_pairs={{0,4},{4,0},{8,12},{12,8},{16,20},{20,16},{24,28},{28,24},{1,5},{5... | collective-permute-start | bytes 2752520 | tf_op jit(solution)/shard_map/ppermute | solution.py:10
  10.5 11.0 %copy-start.10 = (bf16[64,4096]{1,0:T(8,128)(2,1)S(1)}, bf16[64,4096]{1,0:T(8,128)(2,1)}, u32[]{:S(2)}) copy-start(bf16[64,4096]{1,0:T(8,128)(2,1)} %param.19) | copy-start | bytes 1572868
  10.5 11.8 %copy-start.4 = (bf16[1,128,3584]{2,1,0:T(8,128)(2,1)S(1)}, bf16[1,128,3584]{2,1,0:T(8,128)(2,1)}, u32[]{:S(2)}) copy-start(bf16[1,128,3584]{2,1,0:T(8,128)(2,1)} %param.17) | copy-start | bytes 2752516
  22.3 112.7 %reduce-scatter.2.cloned.1.call-start = ((), (), s32[]{:S(2)}) async-start(), calls=%async_computation.1 | async-start | bytes 2621440 | tf_op jit(solution)/shard_map/reduce_scatter | solution.py:24
  23.7 0.9 copy-start.8
  23.7 30.3 %copy-start.6 = (bf16[128,3584]{1,0:T(8,128)(2,1)}, bf16[128,3584]{1,0:T(8,128)(2,1)S(1)}, u32[]{:S(2)}) copy-start(bf16[128,3584]{1,0:T(8,128)(2,1)S(1)} %get-tuple-element.8) | copy-start | bytes 2752516
  23.7 1.8 %copy-start.5 = (bf16[1,128,3584]{2,1,0:T(8,128)(2,1)S(1)}, bf16[1,128,3584]{2,1,0:T(8,128)(2,1)}, u32[]{:S(2)}) copy-start(bf16[1,128,3584]{2,1,0:T(8,128)(2,1)} %param.14) | copy-start | bytes 2752516
  54.0 29.3 %copy-start.12 = (f32[1,2048]{1,0:T(1,128)S(1)}, f32[1,2048]{1,0:T(1,128)}, u32[]{:S(2)}) copy-start(f32[1,2048]{1,0:T(1,128)} %param.13) | copy-start | bytes 24580
  54.0 30.0 %copy-start.9 = (bf16[128,3584]{1,0:T(8,128)(2,1)S(1)}, bf16[128,3584]{1,0:T(8,128)(2,1)}, u32[]{:S(2)}) copy-start(bf16[128,3584]{1,0:T(8,128)(2,1)} %get-tuple-element.11) | copy-start | bytes 2752516
  92.9 1.2 copy-start.3
  101.8 1.8 %copy-start.1 = (f32[256,3584]{1,0:T(8,128)}, f32[256,3584]{1,0:T(8,128)S(1)}, u32[]{:S(2)}) copy-start(f32[256,3584]{1,0:T(8,128)S(1)} %fusion.7) | copy-start | bytes 11010052
  103.6 1.4 copy-start.13
  104.9 7.2 %collective-permute-start.6 = (f32[128,3584]{1,0:T(8,128)}, f32[128,3584]{1,0:T(8,128)S(1)}, u32[]{:S(2)}, u32[]{:S(2)}) collective-permute-start(f32[128,3584]{1,0:T(8,128)} %constant_dynamic-slice_fusion), channel_id=1, source_target_pairs={{0,4},{4,0},{8,12},{12,8},{16,20},{20,16},{24,28},{28,24},{1,5},{5... | collective-permute-start | bytes 5505032 | tf_op jit(solution)/shard_map/ppermute | solution.py:10
  105.0 9.6 %collective-permute-start = (bf16[64,2048]{1,0:T(8,128)(2,1)S(1)}, bf16[64,2048]{1,0:T(8,128)(2,1)S(1)}, u32[]{:S(2)}, u32[]{:S(2)}) collective-permute-start(bf16[64,2048]{1,0:T(8,128)(2,1)S(1)} %bitcast.41), channel_id=1, source_target_pairs={{0,8},{4,12},{8,16},{12,20},{16,24},{20,28},{1,9},{5,13},{9,17},{1... | collective-permute-start | bytes 786440 | tf_op jit(solution)/shard_map/ppermute | solution.py:16
  108.4 1.6 %copy-start.7 = (bf16[128,3584]{1,0:T(8,128)(2,1)S(1)}, bf16[128,3584]{1,0:T(8,128)(2,1)}, u32[]{:S(2)}) copy-start(bf16[128,3584]{1,0:T(8,128)(2,1)} %copy-done.6) | copy-start | bytes 2752516
  108.7 3.4 %copy-start.2 = (f32[256,3584]{1,0:T(8,128)S(1)}, f32[256,3584]{1,0:T(8,128)}, u32[]{:S(2)}) copy-start(f32[256,3584]{1,0:T(8,128)} %copy-done.1) | copy-start | bytes 11010052
  108.7 1.2 collective-permute-start.5
  112.1 22.8 %copy-start.11 = (bf16[64,4096]{1,0:T(8,128)(2,1)S(1)}, bf16[64,4096]{1,0:T(8,128)(2,1)}, u32[]{:S(2)}) copy-start(bf16[64,4096]{1,0:T(8,128)(2,1)} %param.16) | copy-start | bytes 1572868
Sparse Core Ops, SparseCore 0:
  22.4 31.5 all-gather.1
  93.0 41.9 reduce-scatter.1
where the time goes:
time: 144 us
  waiting for transfers between devices  49.1 us (34%)
  matrix products  41.4 us (29%)
  blocking collectives  19.6 us (14%)
  between operations  14.2 us (10%)
  other arithmetic  7.57 us (5%)
  starting transfers between devices  6.09 us (4%)
  local copies, waits for them, and re-layouts  5.62 us (4%)
    all_gather x1, waiting for transfers between devices, local(): cot_block = lax.all_gather(cotangent, 'tensor', axis=0, tiled=True)  27.4 us
    reduce_scatter x1, waiting for transfers between devices, forward_rows(): lax.psum_scatter(term_fn(jnp.int32(0), own_rows * lax.axis_size('tensor')...  20.4 us
    psum x1, blocking collectives, column_norms(): return jnp.sqrt(lax.psum(squares, 'tensor') + epsilon)  19.6 us
    dot_general x1, matrix products, local(): jnp.einsum('rf,rd->fd', fac_a, fac_b, preferred_element_type=jnp.float32)  11 us
    dot_general x1, matrix products, local(): recomputed = jnp.dot(hid_bwd, merged, preferred_element_type=jnp.float32)  9.7 us
    dot_general x1, matrix products, scaled_term(): jnp.dot(hid_fwd, merged, preferred_element_type=jnp.float32) * col_scale  8.91 us
    dot_general x1, matrix products, local(): jnp.einsum('td,fd->tf', scaled_cot, merged, preferred_element_type=jnp.fl...  7.7 us
    ppermute x2, starting transfers between devices, from_behind(): return lax.ppermute(array, axis, pairs)  4.65 us
  transfers between devices with their start and end apart: 9, of which 3 were waited for; matrix products, arithmetic and copies ran while one was open for 20% of the time, Pallas kernels for 0%

commit v1 on v0

--- a/solution.py
+++ b/solution.py
@@ -4,6 +4,16 @@
 from jax.sharding import PartitionSpec as P
 
 epsilon = 1e-06
+
+
+def turned_line(value, axis, dim):
+    count = lax.axis_size(axis)
+    current, pieces = (value, [value])
+    for _ in range(count - 1):
+        current = lax.ppermute(current, axis, [(i, (i + 1) % count) for i in range(count)])
+        pieces.insert(0, current)
+    flat = jnp.concatenate(pieces, axis=dim)
+    return jnp.roll(flat, (lax.axis_index(axis) + 1) * value.shape[dim], axis=dim)
 
 
 def swapped(array, axis, apart):
@@ -86,7 +96,7 @@
     projected = forward_rows(scaled_term, own_rows)
     section_out = (inflow.astype(jnp.float32) + projected).astype(jnp.bfloat16)
     all_rows = hid_bwd.shape[0]
-    cot_block = lax.all_gather(cotangent, "tensor", axis=0, tiled=True)
+    cot_block = turned_line(cotangent, "tensor", 0)
     scaled_cot = (cot_block.astype(jnp.float32) * col_scale).astype(jnp.bfloat16)
     hid_part = jnp.einsum("td,fd->tf", scaled_cot, merged, preferred_element_type=jnp.float32)
     hid_acc = hid_part

time: 144 us -> 139 us (0.965)
  waiting for transfers between devices: 49.1 us -> 40.7 us
  starting transfers between devices: 6.09 us -> 10 us
  matrix products: 41.4 us -> 43.7 us
  local copies, waits for them, and re-layouts: 5.62 us -> 3.37 us
    all_gather x1 -> x0, waiting for transfers between devices: 27.4 us -> none  [local(): cot_block = lax.all_gather(cotangent, 'tensor', axis=0, tiled=True)]
    ppermute x0 -> x3, waiting for transfers between devices: none -> 11.5 us  [turned_line(): lax.ppermute(current, axis, [(i, (i + 1) % count) for i in range(count)])]
    ppermute x2, waiting for transfers between devices: 1.2 us -> 9.02 us  [from_behind(): return lax.ppermute(array, axis, pairs)]
    ppermute x0 -> x3, starting transfers between devices: none -> 3.15 us  [turned_line(): lax.ppermute(current, axis, [(i, (i + 1) % count) for i in range(count)])]
    unnamed x28 -> x31, local copies, waits for them, and re-layouts: 4.24 us -> 1.96 us
    dot_general x1, matrix products: 8.91 us -> 10.7 us  [scaled_term(): jnp.dot(hid_fwd, merged, preferred_element_type=jnp.float32) * col_scale]
  transfers between devices with their start and end apart: 9 -> 11, of which waited for: 3 -> 4; matrix products, arithmetic and copies ran while one was open for 20% -> 22% of each run, Pallas kernels for 0% -> 0%
where the time goes in v1:
time: 139 us
  matrix products  43.7 us (31%)
  waiting for transfers between devices  40.7 us (29%)
  blocking collectives  19.6 us (14%)
  between operations  14.3 us (10%)
  starting transfers between devices  10 us (7%)
  other arithmetic  7.07 us (5%)
  local copies, waits for them, and re-layouts  3.37 us (2%)
    reduce_scatter x1, waiting for transfers between devices, forward_rows(): lax.psum_scatter(term_fn(jnp.int32(0), own_rows * lax.axis_size('tensor')...  20.1 us
    psum x1, blocking collectives, column_norms(): return jnp.sqrt(lax.psum(squares, 'tensor') + epsilon)  19.6 us
    ppermute x3, waiting for transfers between devices, turned_line(): lax.ppermute(current, axis, [(i, (i + 1) % count) for i in range(count)])  11.5 us
    dot_general x1, matrix products, local(): jnp.einsum('rf,rd->fd', fac_a, fac_b, preferred_element_type=jnp.float32)  10.9 us
    dot_general x1, matrix products, scaled_term(): jnp.dot(hid_fwd, merged, preferred_element_type=jnp.float32) * col_scale  10.7 us
    ppermute x2, waiting for transfers between devices, from_behind(): return lax.ppermute(array, axis, pairs)  9.02 us
    dot_general x1, matrix products, local(): recomputed = jnp.dot(hid_bwd, merged, preferred_element_type=jnp.float32)  8.39 us
    dot_general x1, matrix products, local(): jnp.einsum('td,fd->tf', scaled_cot, merged, preferred_element_type=jnp.fl...  8.01 us
  transfers between devices with their start and end apart: 11, of which 4 were waited for; matrix products, arithmetic and copies ran while one was open for 22% of the time, Pallas kernels for 0%

profile of v1, /device:TPU:0, one launch (start us, length us, event | category | flops | bytes accessed | tf_op | source)
XLA Modules:
  0.0 138.7 jit_solution(6988960764178052782)
XLA Ops:
  7.2 1.3 collective-permute-start.3
  9.6 9.0 %collective-permute-done.3 = bf16[64,2048]{1,0:T(8,128)(2,1)S(1)} collective-permute-done((bf16[64,2048]{1,0:T(8,128)(2,1)}, bf16[64,2048]{1,0:T(8,128)(2,1)S(1)}, u32[]{:S(2)}, u32[]{:S(2)}) %collective-permute-start.3) | collective-permute-done | bytes 262176 | tf_op jit(solution)/shard_map/ppermute | solution.py:26
  18.6 1.0 dynamic-slice_select_fusion
  19.6 1.9 %collective-permute-start.4 = (bf16[64,2048]{1,0:T(8,128)(2,1)S(1)}, bf16[64,2048]{1,0:T(8,128)(2,1)S(1)}, u32[]{:S(2)}, u32[]{:S(2)}) collective-permute-start(bf16[64,2048]{1,0:T(8,128)(2,1)S(1)} %dynamic-slice_select_fusion), channel_id=1, source_target_pairs={{0,1},{1,2},{2,3},{3,0},{4,5},{5,6},{6,7},{7,4},{8,9},{9,10},{10,1... | collective-permute-start | bytes 786440 | tf_op jit(solution)/shard_map/ppermute | solution.py:13
  21.5 0.8 broadcast_select_fusion.5
  22.3 6.6 %collective-permute-done.4 = bf16[64,2048]{1,0:T(8,128)(2,1)S(1)} collective-permute-done((bf16[64,2048]{1,0:T(8,128)(2,1)S(1)}, bf16[64,2048]{1,0:T(8,128)(2,1)S(1)}, u32[]{:S(2)}, u32[]{:S(2)}) %collective-permute-start.4) | collective-permute-done | bytes 262176 | tf_op jit(solution)/shard_map/ppermute | solution.py:13
  29.0 10.9 %multiply_reduce_fusion = (f32[2048]{0:T(1024)S(1)}, bf16[3584,2048]{1,0:T(8,128)(2,1)}) fusion(bf16[1,16,2048]{2,1,0:T(8,128)(2,1)S(1)} %copy-done, bf16[8,3584]{1,0:T(8,128)(2,1)S(1)} %get-tuple-element.13, bf16[8,3584]{1,0:T(8,128)(2,1)S(1)} %get-tuple-element.12, bf16[1,3584,2048]{2,1,0:T(8,128)(2,1)} %param.10), kind=kOutput, calls=%fused_computation.2 | convolution fusion | flops 279148544 | bytes 29548544 | tf_op jit(solution)/shard_map/rf,rd->fd/dot_general | solution.py:84
  39.9 1.3 collective-permute-start.6
  41.2 1.4 broadcast_select_fusion.3
  43.4 4.9 %collective-permute-done.6 = bf16[64,2048]{1,0:T(8,128)(2,1)S(1)} collective-permute-done((bf16[64,2048]{1,0:T(8,128)(2,1)S(1)}, bf16[64,2048]{1,0:T(8,128)(2,1)S(1)}, u32[]{:S(2)}, u32[]{:S(2)}) %collective-permute-start.6) | collective-permute-done | bytes 262176 | tf_op jit(solution)/shard_map/ppermute | solution.py:13
  48.6 8.4 %fusion.5 = f32[2048]{0:T(1024)S(1)} fusion(bf16[3584,2048]{1,0:T(8,128)(2,1)} %get-tuple-element.17, bf16[512,2048]{1,0:T(8,128)(2,1)S(1)} %constant_dynamic-update-slice_fusion, s32[]{:T(128)S(6)} %select_n.91, bf16[128,3584]{1,0:T(8,128)(2,1)S(1)} %get-tuple-element.9, bf16[128,3584]{1,0:T(8,128)(2,1)S(1)} %get-tuple-element.8), kind=kOutput, calls=%fused_computation.14 | convolution fusion | flops 3763337216 | bytes 17571844 | tf_op jit(solution)/shard_map/dot_general | solution.py:106
  57.0 19.6 %all-reduce = (f32[2048]{0:T(1024)S(1)}, f32[2048]{0:T(1024)S(1)}, bf16[256,16]{1,0:T(8,128)(2,1)S(1)}) all-reduce(f32[2048]{0:T(1024)S(1)} %get-tuple-element.16, f32[2048]{0:T(1024)S(1)} %fusion.5, f32[256,16]{1,0:T(8,128)S(1)} %fusion.12), channel_id=1, replica_groups=mesh['section'=8,'tensor'=4] {'tensor'}, use_global_device_ids=true, to_apply=%region_1.2 | all-reduce | flops 8192 | bytes 57344 | tf_op jit(solution)/shard_map/psum | solution.py:30
  76.6 0.6 fusion.18
  77.2 10.7 %convolution_multiply_fusion.1 = f32[256,2048]{1,0:T(8,128)} fusion(bf16[3584,2048]{1,0:T(8,128)(2,1)} %get-tuple-element.17, bf16[128,3584]{1,0:T(8,128)(2,1)} %get-tuple-element.11, bf16[128,3584]{1,0:T(8,128)(2,1)S(1)} %copy-done.7, f32[2048]{0:T(1024)S(1)} %get-tuple-element.15), kind=kOutput, calls=%fused_computation.5 | convolution fusion | flops 3762290688 | bytes 18620416 | tf_op jit(solution)/shard_map/dot_general | solution.py:94
  88.0 8.0 %fusion.7 = f32[256,3584]{1,0:T(8,128)S(1)} fusion(bf16[3584,2048]{1,0:T(8,128)(2,1)} %get-tuple-element.17, f32[2048]{0:T(1024)S(1)} %get-tuple-element.15, bf16[512,2048]{1,0:T(8,128)(2,1)} %copy-done.8, s32[]{:T(128)S(6)} %select_n.91), kind=kOutput, calls=%fused_computation.20 | convolution fusion | flops 3759669248 | bytes 19406852 | tf_op jit(solution)/shard_map/td,fd->tf/dot_general | solution.py:101
  96.0 1.8 %copy-done.1 = f32[256,3584]{1,0:T(8,128)} copy-done((f32[256,3584]{1,0:T(8,128)}, f32[256,3584]{1,0:T(8,128)S(1)}, u32[]{:S(2)}) %copy-start.1) | copy-done | bytes 3670040
  97.8 1.4 %constant_dynamic-slice_fusion = f32[128,3584]{1,0:T(8,128)} fusion(f32[256,3584]{1,0:T(8,128)S(1)} %fusion.7, s32[]{:T(128)S(6)} %select_n.96), kind=kLoop, calls=%fused_computation.48 | loop fusion | bytes 3670020 | tf_op jit(solution)/shard_map/dynamic_slice | solution.py:110
  99.2 4.2 %collective-permute-start = (bf16[64,2048]{1,0:T(8,128)(2,1)S(1)}, bf16[64,2048]{1,0:T(8,128)(2,1)S(1)}, u32[]{:S(2)}, u32[]{:S(2)}) collective-permute-start(bf16[64,2048]{1,0:T(8,128)(2,1)S(1)} %bitcast.41), channel_id=1, source_target_pairs={{0,8},{4,12},{8,16},{12,20},{16,24},{20,28},{1,9},{5,13},{9,17},{1... | collective-permute-start | bytes 786440 | tf_op jit(solution)/shard_map/ppermute | solution.py:26
  103.4 1.7 %fusion.10 = f32[256,16]{0,1:T(8,128)S(1)} fusion(f32[2048]{0:T(1024)S(1)} %get-tuple-element.15, bf16[512,2048]{1,0:T(8,128)(2,1)} %copy-done.8, s32[]{:T(128)S(6)} %select_n.91, bf16[1,16,2048]{2,1,0:T(8,128)(2,1)S(1)} %copy-done), kind=kOutput, calls=%fused_computation.21 | convolution fusion | flops 18350080 | bytes 1138692 | tf_op jit(solution)/shard_map/td,rd->tr/dot_general | solution.py:103
  105.4 2.3 %convolution_bitcast_fusion.1 = f32[1,16,2048]{2,1,0:T(8,128)} fusion(f32[2048]{0:T(1024)S(1)} %get-tuple-element.15, bf16[512,2048]{1,0:T(8,128)(2,1)} %copy-done.8, s32[]{:T(128)S(6)} %select_n.91, bf16[256,16]{1,0:T(8,128)(2,1)S(1)} %get-tuple-element.7), kind=kOutput, calls=%fused_computation.7 | convolution fusion | flops 18350080 | bytes 1196036 | tf_op jit(solution)/shard_map/tr,td->rd/dot_general | solution.py:105
  107.7 1.0 convolution_bitcast_fusion
  108.7 1.2 fusion.6
  109.9 20.1 %reduce-scatter.2.cloned.1.call-done = f32[64,2048]{1,0:T(8,128)} async-done(((f32[256,2048]{1,0:T(8,128)}), f32[64,2048]{1,0:T(8,128)}) %reduce-scatter.2.cloned.1.call-update) | async-done | bytes 524304 | tf_op jit(solution)/shard_map/reduce_scatter | solution.py:34
  130.0 1.8 %fusion.13 = bf16[1,64,2048]{2,1,0:T(8,128)(2,1)} fusion(f32[64,2048]{1,0:T(8,128)} %reduce-scatter.2.cloned.1.call-done, bf16[64,2048]{1,0:T(8,128)(2,1)S(1)} %collective-permute-done, bf16[64,4096]{1,0:T(8,128)(2,1)S(1)} %copy-done.9, s32[]{:T(128)S(6)} %select_n.80, pred[]{:T(512)S(6)} %lt.34), kind=kLoop, calls=%fused_computation.24 | loop fusion | flops 524288 | bytes 1310725 | tf_op jit(solution)/shard_map/broadcast_in_dim | solution.py:119
  (48 shorter events, 2.4 us)
Async XLA Ops:
  7.2 21.8 %copy-start = (bf16[1,16,2048]{2,1,0:T(8,128)(2,1)S(1)}, bf16[1,16,2048]{2,1,0:T(8,128)(2,1)}, u32[]{:S(2)}) copy-start(bf16[1,16,2048]{2,1,0:T(8,128)(2,1)} %param.12) | copy-start | bytes 196612
  7.2 122.8 %reduce-scatter.2.cloned.1.call-start = ((), (), s32[]{:S(2)}) async-start(), calls=%async_computation.1 | async-start | bytes 2621440 | tf_op jit(solution)/shard_map/reduce_scatter | solution.py:34
  7.2 11.4 %collective-permute-start.3 = (bf16[64,2048]{1,0:T(8,128)(2,1)}, bf16[64,2048]{1,0:T(8,128)(2,1)S(1)}, u32[]{:S(2)}, u32[]{:S(2)}) collective-permute-start(bf16[64,2048]{1,0:T(8,128)(2,1)} %bitcast.40), channel_id=1, source_target_pairs={{8,0},{12,4},{16,8},{20,12},{24,16},{28,20},{9,1},{13,5},{17,9},{2... | collective-permute-start | bytes 786440 | tf_op jit(solution)/shard_map/ppermute | solution.py:26
  8.5 13.0 %collective-permute-start.2 = (bf16[8,3584]{1,0:T(8,128)(2,1)}, bf16[8,3584]{1,0:T(8,128)(2,1)S(1)}, u32[]{:S(2)}, u32[]{:S(2)}) collective-permute-start(bf16[8,3584]{1,0:T(8,128)(2,1)} %bitcast.37), channel_id=1, source_target_pairs={{0,4},{4,0},{8,12},{12,8},{16,20},{20,16},{24,28},{28,24},{1,5},{5... | collective-permute-start | bytes 172040 | tf_op jit(solution)/shard_map/ppermute | solution.py:20
  9.1 32.1 %collective-permute-start.1 = (bf16[128,3584]{1,0:T(8,128)(2,1)}, bf16[128,3584]{1,0:T(8,128)(2,1)S(1)}, u32[]{:S(2)}, u32[]{:S(2)}) collective-permute-start(bf16[128,3584]{1,0:T(8,128)(2,1)} %bitcast.35), channel_id=1, source_target_pairs={{0,4},{4,0},{8,12},{12,8},{16,20},{20,16},{24,28},{28,24},{1,5},{5... | collective-permute-start | bytes 2752520 | tf_op jit(solution)/shard_map/ppermute | solution.py:20
  9.2 33.4 %collective-permute-start.7 = (bf16[128,3584]{1,0:T(8,128)(2,1)}, bf16[128,3584]{1,0:T(8,128)(2,1)S(1)}, u32[]{:S(2)}, u32[]{:S(2)}) collective-permute-start(bf16[128,3584]{1,0:T(8,128)(2,1)} %bitcast.36), channel_id=1, source_target_pairs={{0,4},{4,0},{8,12},{12,8},{16,20},{20,16},{24,28},{28,24},{1,5},{5... | collective-permute-start | bytes 2752520 | tf_op jit(solution)/shard_map/ppermute | solution.py:20
  19.6 9.3 %collective-permute-start.4 = (bf16[64,2048]{1,0:T(8,128)(2,1)S(1)}, bf16[64,2048]{1,0:T(8,128)(2,1)S(1)}, u32[]{:S(2)}, u32[]{:S(2)}) collective-permute-start(bf16[64,2048]{1,0:T(8,128)(2,1)S(1)} %dynamic-slice_select_fusion), channel_id=1, source_target_pairs={{0,1},{1,2},{2,3},{3,0},{4,5},{5,6},{6,7},{7,4},{8,9},{9,10},{10,1... | collective-permute-start | bytes 786440 | tf_op jit(solution)/shard_map/ppermute | solution.py:13
  29.0 11.0 %collective-permute-start.5 = (bf16[64,2048]{1,0:T(8,128)(2,1)S(1)}, bf16[64,2048]{1,0:T(8,128)(2,1)S(1)}, u32[]{:S(2)}, u32[]{:S(2)}) collective-permute-start(bf16[64,2048]{1,0:T(8,128)(2,1)S(1)} %collective-permute-done.4), channel_id=1, source_target_pairs={{0,1},{1,2},{2,3},{3,0},{4,5},{5,6},{6,7},{7,4},{8,9},{9,10},{10,1... | collective-permute-start | bytes 786440 | tf_op jit(solution)/shard_map/ppermute | solution.py:13
  29.0 12.2 %copy-start.3 = (bf16[1,128,3584]{2,1,0:T(8,128)(2,1)S(1)}, bf16[1,128,3584]{2,1,0:T(8,128)(2,1)}, u32[]{:S(2)}) copy-start(bf16[1,128,3584]{2,1,0:T(8,128)(2,1)} %param.14) | copy-start | bytes 2752516
  39.9 2.7 %copy-start.4 = (bf16[1,128,3584]{2,1,0:T(8,128)(2,1)S(1)}, bf16[1,128,3584]{2,1,0:T(8,128)(2,1)}, u32[]{:S(2)}) copy-start(bf16[1,128,3584]{2,1,0:T(8,128)(2,1)} %param.17) | copy-start | bytes 2752516
  39.9 8.4 %collective-permute-start.6 = (bf16[64,2048]{1,0:T(8,128)(2,1)S(1)}, bf16[64,2048]{1,0:T(8,128)(2,1)S(1)}, u32[]{:S(2)}, u32[]{:S(2)}) collective-permute-start(bf16[64,2048]{1,0:T(8,128)(2,1)S(1)} %collective-permute-done.5), channel_id=1, source_target_pairs={{0,1},{1,2},{2,3},{3,0},{4,5},{5,6},{6,7},{7,4},{8,9},{9,10},{10,1... | collective-permute-start | bytes 786440 | tf_op jit(solution)/shard_map/ppermute | solution.py:13
  42.8 5.7 %copy-start.5 = (bf16[128,3584]{1,0:T(8,128)(2,1)}, bf16[128,3584]{1,0:T(8,128)(2,1)S(1)}, u32[]{:S(2)}) copy-start(bf16[128,3584]{1,0:T(8,128)(2,1)S(1)} %get-tuple-element.9) | copy-start | bytes 2752516
  48.5 8.4 %copy-start.8 = (bf16[512,2048]{1,0:T(8,128)(2,1)}, bf16[512,2048]{1,0:T(8,128)(2,1)S(1)}, u32[]{:S(2)}) copy-start(bf16[512,2048]{1,0:T(8,128)(2,1)S(1)} %constant_dynamic-update-slice_fusion) | copy-start | bytes 6291460
  48.6 28.0 %copy-start.10 = (f32[1,2048]{1,0:T(1,128)S(1)}, f32[1,2048]{1,0:T(1,128)}, u32[]{:S(2)}) copy-start(f32[1,2048]{1,0:T(1,128)} %param.13) | copy-start | bytes 24580
  48.6 28.6 %copy-start.7 = (bf16[128,3584]{1,0:T(8,128)(2,1)S(1)}, bf16[128,3584]{1,0:T(8,128)(2,1)}, u32[]{:S(2)}) copy-start(bf16[128,3584]{1,0:T(8,128)(2,1)} %get-tuple-element.10) | copy-start | bytes 2752516
  96.0 1.8 %copy-start.1 = (f32[256,3584]{1,0:T(8,128)}, f32[256,3584]{1,0:T(8,128)S(1)}, u32[]{:S(2)}) copy-start(f32[256,3584]{1,0:T(8,128)S(1)} %fusion.7) | copy-start | bytes 11010052
  97.8 1.4 %copy-start.11 = (bf16[1,64,2048]{2,1,0:T(8,128)(2,1)S(1)}, bf16[1,64,2048]{2,1,0:T(8,128)(2,1)}, u32[]{:S(2)}) copy-start(bf16[1,64,2048]{2,1,0:T(8,128)(2,1)} %param.15) | copy-start | bytes 786436
  99.2 9.5 %collective-permute-start.9 = (f32[128,3584]{1,0:T(8,128)}, f32[128,3584]{1,0:T(8,128)S(1)}, u32[]{:S(2)}, u32[]{:S(2)}) collective-permute-start(f32[128,3584]{1,0:T(8,128)} %constant_dynamic-slice_fusion), channel_id=1, source_target_pairs={{0,4},{4,0},{8,12},{12,8},{16,20},{20,16},{24,28},{28,24},{1,5},{5... | collective-permute-start | bytes 5505032 | tf_op jit(solution)/shard_map/ppermute | solution.py:20
  99.2 10.7 %collective-permute-start = (bf16[64,2048]{1,0:T(8,128)(2,1)S(1)}, bf16[64,2048]{1,0:T(8,128)(2,1)S(1)}, u32[]{:S(2)}, u32[]{:S(2)}) collective-permute-start(bf16[64,2048]{1,0:T(8,128)(2,1)S(1)} %bitcast.41), channel_id=1, source_target_pairs={{0,8},{4,12},{8,16},{12,20},{16,24},{20,28},{1,9},{5,13},{9,17},{1... | collective-permute-start | bytes 786440 | tf_op jit(solution)/shard_map/ppermute | solution.py:26
  103.4 4.3 %copy-start.6 = (bf16[128,3584]{1,0:T(8,128)(2,1)S(1)}, bf16[128,3584]{1,0:T(8,128)(2,1)}, u32[]{:S(2)}) copy-start(bf16[128,3584]{1,0:T(8,128)(2,1)} %copy-done.5) | copy-start | bytes 2752516
  105.1 3.6 %copy-start.2 = (f32[256,3584]{1,0:T(8,128)S(1)}, f32[256,3584]{1,0:T(8,128)}, u32[]{:S(2)}) copy-start(f32[256,3584]{1,0:T(8,128)} %copy-done.1) | copy-start | bytes 11010052
  105.1 2.6 %collective-permute-start.8 = (f32[256,16]{0,1:T(8,128)S(1)}, f32[256,16]{0,1:T(8,128)S(1)}, u32[]{:S(2)}, u32[]{:S(2)}) collective-permute-start(f32[256,16]{0,1:T(8,128)S(1)} %fusion.10), channel_id=1, source_target_pairs={{0,4},{4,0},{8,12},{12,8},{16,20},{20,16},{24,28},{28,24},{1,5},{5... | collective-permute-start | bytes 49160 | tf_op jit(solution)/shard_map/ppermute | solution.py:20
  108.7 21.3 %copy-start.9 = (bf16[64,4096]{1,0:T(8,128)(2,1)S(1)}, bf16[64,4096]{1,0:T(8,128)(2,1)}, u32[]{:S(2)}) copy-start(bf16[64,4096]{1,0:T(8,128)(2,1)} %param.16) | copy-start | bytes 1572868
Sparse Core Ops, SparseCore 0:
  88.1 41.8 reduce-scatter.1
